TPU v7x, 32 devices: a whole 2x2x4 slice. The times are simulated.
32 devices in a mesh: fsdp: 2 (over x), context: 4 (over y, core), tensor: 4 (over z).
Axes of the slice: x: 2, y: 2, z: 4, core: 2. Of those that a mesh axis runs over, the one named last changes fastest.
Arguments:
- hidden_in: bfloat16 [2, 1024, 2048], P('fsdp', ('context', 'tensor')), may hold values from -6 to 6
- segment_ids: int32 [2, 1024], P('fsdp'), may hold values from 0 to 15, never falling along the last dimension, each value on 1 to 512 neighbouring positions
- pad_mask: int32 [2, 1024], P('fsdp'), may hold values from 0 to 1, as said below
- attn_gain: bfloat16 [2048], P(('fsdp', 'context')), may hold values from 0.5 to 1.5
- w_query: bfloat16 [2048, 2048], P(('fsdp', 'context'), 'tensor'), may hold values from -0.1875 to 0.1875
- w_key: bfloat16 [2048, 256], P(('fsdp', 'context'), 'tensor'), may hold values from -0.1875 to 0.1875
- w_value: bfloat16 [2048, 256], P(('fsdp', 'context'), 'tensor'), may hold values from -0.125 to 0.125
- w_out: bfloat16 [2048, 2048], P('tensor', ('fsdp', 'context')), may hold values from -0.5 to 0.5
- mlp_gain: bfloat16 [2048], P(('fsdp', 'context')), may hold values from 0.5 to 1.5
- w_gate: bfloat16 [2048, 5632], P(('fsdp', 'context'), 'tensor'), may hold values from -0.125 to 0.125
- w_up: bfloat16 [2048, 5632], P(('fsdp', 'context'), 'tensor'), may hold values from -0.125 to 0.125
- w_down: bfloat16 [5632, 2048], P('tensor', ('fsdp', 'context')), may hold values from -0.078125 to 0.078125
- cotangent: bfloat16 [2, 1024, 2048], P('fsdp', ('context', 'tensor')), may hold values from -6 to 6
Outputs:
- block_out: bfloat16 [2, 1024, 2048], P('fsdp', ('context', 'tensor'))
- grad_hidden: float32 [2, 1024, 2048], P('fsdp', ('context', 'tensor'))
- grad_attn_gain: float32 [2048], P(('fsdp', 'context'))
- grad_query: float32 [2048, 2048], P(('fsdp', 'context'), 'tensor')
- grad_key: float32 [2048, 256], P(('fsdp', 'context'), 'tensor')
- grad_value: float32 [2048, 256], P(('fsdp', 'context'), 'tensor')
- grad_out: float32 [2048, 2048], P('tensor', ('fsdp', 'context'))
- grad_mlp_gain: float32 [2048], P(('fsdp', 'context'))
- grad_gate: float32 [2048, 5632], P(('fsdp', 'context'), 'tensor')
- grad_up: float32 [2048, 5632], P(('fsdp', 'context'), 'tensor')
- grad_down: float32 [5632, 2048], P('tensor', ('fsdp', 'context'))
Inputs may be any that keep to these rules, and one draw needn't show every extreme that they name: `segment_ids`: ids never fall along a sequence; a document is a run of 1 to 512 consecutive tokens of one id. `pad_mask`: every sequence ends in one or more padding slots, and no other slot is padding.
All inputs are finite; a program needn't handle non-finite values.
Results may differ from a plain program's by a relative error of at most 0.013.
The roundings to bfloat16 on the way count: a program that leaves them out, or rounds other values in their place, can miss the bound.
Values may be sent and summed in bfloat16 or wider, within the bound.
A program may use at most 88 MiB of HBM per device.

v0:
```python
import math
import jax
import jax.numpy as jnp
from jax import lax
from jax.sharding import PartitionSpec as P

EPS = 1e-05
NEG = -1e30
BF = jnp.bfloat16
F32 = jnp.float32


def rope_tables(positions, head_size):
    half_size = head_size // 2
    frequency = jnp.exp(-(jnp.arange(half_size, dtype=F32) * (2.0 / head_size)) * math.log(10000.0))
    angles = positions.astype(F32)[..., None] * frequency
    return (jnp.cos(angles)[..., None, :], jnp.sin(angles)[..., None, :])


def rotate(vectors, cos_table, sin_table):
    half_size = vectors.shape[-1] // 2
    first_half = vectors[..., :half_size]
    second_half = vectors[..., half_size:]
    return jnp.concatenate(
        [
            first_half * cos_table - second_half * sin_table,
            second_half * cos_table + first_half * sin_table,
        ],
        axis=-1,
    )


def mm(a, b, ca=1, cb=0):
    return lax.dot_general(a, b, (((ca,), (cb,)), ((), ())), preferred_element_type=F32)


def rows_gather(x):
    return lax.all_gather(x, "tensor", axis=0, tiled=True)


def rows_sum(x):
    return lax.psum_scatter(x.astype(BF), "tensor", scatter_dimension=0, tiled=True).astype(F32)


FC = ("fsdp", "context")


def gather_w(w, axis=0):
    return lax.all_gather(w, FC, axis=axis, tiled=True)


def scatter_g(g, axis=0):
    return lax.psum_scatter(g.astype(BF), FC, scatter_dimension=axis, tiled=True).astype(F32)


def norm_back(grad_normed, vectors, inv_scale, gain_row):
    unit_rows = vectors * inv_scale
    weighted = grad_normed * gain_row
    grad_gain = jnp.sum(grad_normed * unit_rows, axis=0)
    grad_vectors = inv_scale * (
        weighted - unit_rows * jnp.mean(weighted * unit_rows, axis=-1, keepdims=True)
    )
    return (grad_vectors, grad_gain)


def one_sequence(
    hidden_in,
    segment_ids,
    pad_mask,
    attn_gain,
    w_query,
    w_key,
    w_value,
    w_out,
    mlp_gain,
    w_gate,
    w_up,
    w_down,
    cotangent,
):
    row_count, model_width = hidden_in.shape
    context_count = lax.axis_size("context")
    tensor_count = lax.axis_size("tensor")
    context_index = lax.axis_index("context")
    tensor_index = lax.axis_index("tensor")
    length = segment_ids.shape[0]
    span = length // context_count
    hd = w_key.shape[1]
    start = context_index * span
    seg_span = lax.dynamic_slice_in_dim(segment_ids, start, span, 0)
    columns = jnp.arange(length, dtype=jnp.int32)
    row_at = start + jnp.arange(span, dtype=jnp.int32)
    first = jnp.sum((segment_ids[None, :] < seg_span[:, None]).astype(jnp.int32), axis=1)
    cos_t, sin_t = rope_tables(row_at - first, hd)
    row_start = start + tensor_index * row_count
    keep = lax.dynamic_slice_in_dim(pad_mask, row_start, row_count, 0).astype(F32)[:, None]
    allowed = (
        (seg_span[:, None] == segment_ids[None, :])
        & (columns[None, :] <= row_at[:, None])
        & ((pad_mask[None, :] == 1) | (columns[None, :] == row_at[:, None]))
    )
    gain_one = gather_w(attn_gain).astype(F32)
    gain_two = gather_w(mlp_gain).astype(F32)
    qkv_all = gather_w(jnp.concatenate([w_query, w_key, w_value], axis=1))
    out_all = gather_w(w_out, 1)
    gate_all = gather_w(w_gate)
    up_all = gather_w(w_up)
    down_all = gather_w(w_down, 1)
    qw = w_query.shape[1]
    hidden = hidden_in.astype(F32)
    scale_one = lax.rsqrt(jnp.mean(hidden * hidden, axis=-1, keepdims=True) + EPS)
    n1 = rows_gather((hidden * scale_one * gain_one).astype(BF))
    g_out = cotangent.astype(F32) * keep
    g_all = rows_gather(g_out.astype(BF))
    pre = mm(n1, qkv_all)
    q = rotate(pre[:, :qw].reshape(span, -1, hd), cos_t, sin_t).astype(BF)
    k = rotate(pre[:, None, qw : qw + hd], cos_t, sin_t).astype(BF)[:, 0]
    v = pre[:, qw + hd :].astype(BF)
    kv = lax.all_gather(jnp.concatenate([k, v], axis=1), "context", axis=0, tiled=True)
    k, v = (kv[:, :hd], kv[:, hd:])
    scale = hd ** (-0.5)
    scores = jnp.einsum("qhd,td->hqt", q, k, preferred_element_type=F32) * scale
    scores = jnp.where(allowed[None], scores, NEG)
    top = jnp.max(scores, axis=-1, keepdims=True)
    e = jnp.exp(scores - top)
    probs = e / jnp.sum(e, axis=-1, keepdims=True)
    probs_b = probs.astype(BF)
    attn = jnp.einsum("hqt,td->qhd", probs_b, v, preferred_element_type=F32)
    attn = attn.reshape(span, -1).astype(BF)
    middle = hidden + rows_sum(mm(attn, out_all))
    scale_two = lax.rsqrt(jnp.mean(middle * middle, axis=-1, keepdims=True) + EPS)
    n2 = rows_gather((middle * scale_two * gain_two).astype(BF))
    gate = mm(n2, gate_all)
    up = mm(n2, up_all)
    sig = jax.nn.sigmoid(gate)
    inner = (gate * sig * up).astype(BF)
    block_out = (keep * (middle + rows_sum(mm(inner, down_all)))).astype(BF)
    grad_down = mm(inner, g_all, 0, 0)
    g_inner = mm(g_all, down_all, 1, 1)
    g_gate = (g_inner * up * sig * (1.0 + gate * (1.0 - sig))).astype(BF)
    g_up = (g_inner * gate * sig).astype(BF)
    g_n2 = rows_sum(mm(g_gate, gate_all, 1, 1) + mm(g_up, up_all, 1, 1))
    grad_gate = mm(n2, g_gate, 0, 0)
    grad_up = mm(n2, g_up, 0, 0)
    d_mid, grad_gain_two = norm_back(g_n2, middle, scale_two, gain_two)
    g_mid = g_out + d_mid
    gm_all = rows_gather(g_mid.astype(BF))
    grad_out = mm(attn, gm_all, 0, 0)
    g_attn = mm(gm_all, out_all, 1, 1).astype(BF).reshape(span, -1, hd)
    dp = jnp.einsum("qhd,td->hqt", g_attn, v, preferred_element_type=F32)
    delta = jnp.sum(probs * dp, axis=-1, keepdims=True)
    ds = (probs * (dp - delta)).astype(BF)
    g_q = jnp.einsum("hqt,td->qhd", ds, k, preferred_element_type=F32) * scale
    g_k = jnp.einsum("hqt,qhd->td", ds, q, preferred_element_type=F32) * scale
    g_v = jnp.einsum("hqt,qhd->td", probs_b, g_attn, preferred_element_type=F32)
    g_kv = lax.psum_scatter(
        jnp.concatenate([g_k, g_v], axis=1), "context", scatter_dimension=0, tiled=True
    )
    g_q = rotate(g_q, cos_t, -sin_t).astype(BF).reshape(span, -1)
    g_k = rotate(g_kv[:, None, :hd], cos_t, -sin_t).astype(BF)[:, 0]
    g_qkv = jnp.concatenate([g_q, g_k, g_kv[:, hd:].astype(BF)], axis=1)
    g_n1 = rows_sum(mm(g_qkv, qkv_all, 1, 1))
    grad_qkv = mm(n1, g_qkv, 0, 0)
    d_hid, grad_gain_one = norm_back(g_n1, hidden, scale_one, gain_one)
    gains = jnp.stack([grad_gain_one, grad_gain_two])
    return (block_out, g_mid + d_hid, gains, grad_qkv, grad_out, grad_gate, grad_up, grad_down)


def body(
    hidden_in,
    segment_ids,
    pad_mask,
    attn_gain,
    w_query,
    w_key,
    w_value,
    w_out,
    mlp_gain,
    w_gate,
    w_up,
    w_down,
    cotangent,
):
    block_out, grad_hidden, gains, grad_qkv, grad_out, grad_gate, grad_up, grad_down = one_sequence(
        hidden_in[0],
        segment_ids[0],
        pad_mask[0],
        attn_gain,
        w_query,
        w_key,
        w_value,
        w_out,
        mlp_gain,
        w_gate,
        w_up,
        w_down,
        cotangent[0],
    )
    grad_down = scatter_g(grad_down, 1)
    grad_gate = scatter_g(grad_gate)
    grad_up = scatter_g(grad_up)
    grad_out = scatter_g(grad_out, 1)
    grad_qkv = scatter_g(grad_qkv)
    gains = lax.psum(gains, "tensor")
    gains = lax.psum_scatter(gains, FC, scatter_dimension=1, tiled=True)
    qw, hd = (w_query.shape[1], w_key.shape[1])
    return (
        block_out[None],
        grad_hidden[None],
        gains[0],
        grad_qkv[:, :qw],
        grad_qkv[:, qw : qw + hd],
        grad_qkv[:, qw + hd :],
        grad_out,
        gains[1],
        grad_gate,
        grad_up,
        grad_down,
    )


def solution(mesh):
    fc = ("fsdp", "context")
    rows = P("fsdp", ("context", "tensor"), None)
    tail = (
        P(fc),
        P(fc, "tensor"),
        P(fc, "tensor"),
        P(fc, "tensor"),
        P("tensor", fc),
        P(fc),
        P(fc, "tensor"),
        P(fc, "tensor"),
        P("tensor", fc),
    )
    in_specs = (rows, P("fsdp", None), P("fsdp", None)) + tail + (rows,)
    out_specs = (rows, rows) + tail
    return jax.shard_map(body, mesh=mesh, in_specs=in_specs, out_specs=out_specs, check_vma=False)
```

profile of v0, /device:TPU:0, one launch (start us, length us, event | category | flops | bytes accessed | tf_op | source)
XLA Modules:
  0.0 838.9 jit_solution(12737155059699517862)
XLA Ops:
  7.2 1.1 fusion.43
  9.0 10.3 %all-gather = bf16[8,1,256]{2,1,0:T(2,128)(2,1)S(1)} all-gather(bf16[1,1,256]{2,1,0:T(2,128)(2,1)S(1)} %reshape.348), channel_id=1, replica_groups=mesh['fsdp'=2,'context'=4,'tensor'=4] {'fsdp','context'}, dimensions={0}, use_global_device_ids=true | all-gather | bytes 4608 | tf_op jit(solution)/shard_map/all_gather | solution.py:49
  19.4 1.8 fusion.40
  23.0 1.8 pad_maximum_fusion.1
  28.1 1.7 fusion.22
  29.8 19.8 %all-gather.12.cloned.1.call-done = bf16[256,2048]{1,0:T(8,128)(2,1)} async-done(((bf16[64,2048]{1,0:T(8,128)(2,1)}), bf16[256,2048]{1,0:T(8,128)(2,1)}) %all-gather.12.cloned.1.call-update) | async-done | bytes 1048592 | tf_op jit(solution)/shard_map/all_gather | solution.py:38
  49.6 32.1 %all-gather.14.cloned.1.call-done = bf16[2048,640]{1,0:T(8,128)(2,1)} async-done(((bf16[256,640]{1,0:T(8,128)(2,1)}), bf16[2048,640]{1,0:T(8,128)(2,1)}) %all-gather.14.cloned.1.call-update) | async-done | bytes 2621456 | tf_op jit(solution)/shard_map/all_gather | solution.py:49
  81.7 3.0 fusion.84
  85.8 5.8 all_gather.39
  91.6 4.8 fusion.83
  96.4 4.3 fusion.14
  100.8 11.0 %all-gather.16.cloned.1.call-done = bf16[512,2048]{1,0:T(8,128)(2,1)} async-done(((bf16[512,256]{1,0:T(8,128)(2,1)}), bf16[512,2048]{1,0:T(8,128)(2,1)}) %all-gather.16.cloned.1.call-update) | async-done | bytes 2097168 | tf_op jit(solution)/shard_map/all_gather | solution.py:49
  111.8 3.3 convolution_convert_fusion.5
  115.2 8.8 %all-gather.1 = bf16[8,1,256]{2,1,0:T(2,128)(2,1)S(1)} all-gather(bf16[1,1,256]{2,1,0:T(2,128)(2,1)S(1)} %reshape.350), channel_id=1, replica_groups=mesh['fsdp'=2,'context'=4,'tensor'=4] {'fsdp','context'}, dimensions={0}, use_global_device_ids=true | all-gather | bytes 4608 | tf_op jit(solution)/shard_map/all_gather | solution.py:49
  124.0 18.4 %reduce-scatter.14.cloned.1.call-done = bf16[64,2048]{1,0:T(8,128)(2,1)} async-done(((bf16[256,2048]{1,0:T(8,128)(2,1)}), bf16[64,2048]{1,0:T(8,128)(2,1)}) %reduce-scatter.14.cloned.1.call-update) | async-done | bytes 262160 | tf_op jit(solution)/shard_map/reduce_scatter | solution.py:42
  142.4 1.1 multiply_reduce_fusion
  143.6 1.8 multiply_convert_fusion.4
  149.3 22.8 %all-gather.18.cloned.1.call-done = bf16[256,2048]{1,0:T(8,128)(2,1)} async-done(((bf16[64,2048]{1,0:T(8,128)(2,1)}), bf16[256,2048]{1,0:T(8,128)(2,1)}) %all-gather.18.cloned.1.call-update) | async-done | bytes 1048592 | tf_op jit(solution)/shard_map/all_gather | solution.py:38
  172.1 44.7 %all-gather.22.cloned.1.call-done = bf16[2048,1408]{1,0:T(8,128)(2,1)} async-done(((bf16[256,1408]{1,0:T(8,128)(2,1)}), bf16[2048,1408]{1,0:T(8,128)(2,1)}) %all-gather.22.cloned.1.call-update) | async-done | bytes 5767184 | tf_op jit(solution)/shard_map/all_gather | solution.py:49
  216.8 5.9 fusion.86
  222.7 39.5 %all-gather.20.cloned.1.call-done = bf16[2048,1408]{1,0:T(8,128)(2,1)} async-done(((bf16[256,1408]{1,0:T(8,128)(2,1)}), bf16[2048,1408]{1,0:T(8,128)(2,1)}) %all-gather.20.cloned.1.call-update) | async-done | bytes 5767184 | tf_op jit(solution)/shard_map/all_gather | solution.py:49
  262.2 5.5 fusion.85
  267.8 24.7 %all-gather.26.cloned.1.call-done = bf16[256,2048]{1,0:T(8,128)(2,1)} async-done(((bf16[64,2048]{1,0:T(8,128)(2,1)}), bf16[256,2048]{1,0:T(8,128)(2,1)}) %all-gather.26.cloned.1.call-update) | async-done | bytes 1048592 | tf_op jit(solution)/shard_map/all_gather | solution.py:38
  292.4 45.9 %all-gather.24.cloned.1.call-done = bf16[1408,2048]{1,0:T(8,128)(2,1)} async-done(((bf16[1408,256]{1,0:T(8,128)(2,1)}), bf16[1408,2048]{1,0:T(8,128)(2,1)}) %all-gather.24.cloned.1.call-update) | async-done | bytes 5767184 | tf_op jit(solution)/shard_map/all_gather | solution.py:49
  338.3 6.2 multiply_convert_fusion
  344.6 1.8 fusion.87
  346.5 5.5 fusion.8
  352.0 27.2 %reduce-scatter.18.cloned.1.call-done = bf16[64,2048]{1,0:T(8,128)(2,1)} async-done(((bf16[256,2048]{1,0:T(8,128)(2,1)}), bf16[64,2048]{1,0:T(8,128)(2,1)}) %reduce-scatter.18.cloned.1.call-update) | async-done | bytes 262160 | tf_op jit(solution)/shard_map/reduce_scatter | solution.py:42
  379.3 1.3 fusion.39
  380.6 1.9 fusion.80
  382.8 26.5 %all-gather.28.cloned.1.call-done = bf16[256,2048]{1,0:T(8,128)(2,1)} async-done(((bf16[64,2048]{1,0:T(8,128)(2,1)}), bf16[256,2048]{1,0:T(8,128)(2,1)}) %all-gather.28.cloned.1.call-update) | async-done | bytes 1048592 | tf_op jit(solution)/shard_map/all_gather | solution.py:38
  409.3 3.4 convolution_convert_fusion.8
  412.7 1.8 copy.92
  414.4 4.9 fusion.17
  419.4 4.8 fusion.1
  424.3 1.2 fusion.3
  425.5 1.9 copy-done
  427.4 1.4 fusion.20
  429.7 3.1 fusion.13
  432.9 18.1 %reduce-scatter.20.cloned.1.call-done = f32[256,128]{0,1:T(8,128)} async-done(((f32[1024,128]{0,1:T(8,128)}), f32[256,128]{0,1:T(8,128)}) %reduce-scatter.20.cloned.1.call-update) | async-done | bytes 131088 | tf_op jit(solution)/shard_map/reduce_scatter | solution.py:156
  452.9 3.7 convolution_convert_fusion.6
  456.7 3.3 convolution_convert_fusion.4
  460.1 5.4 convolution_convert_fusion.7
  465.6 18.3 %reduce-scatter.22.cloned.1.call-done = bf16[64,2048]{1,0:T(8,128)(2,1)} async-done(((bf16[256,2048]{1,0:T(8,128)(2,1)}), bf16[64,2048]{1,0:T(8,128)(2,1)}) %reduce-scatter.22.cloned.1.call-update) | async-done | bytes 262160 | tf_op jit(solution)/shard_map/reduce_scatter | solution.py:42
  484.0 1.3 fusion.42
  485.2 1.3 copy.112
  486.7 2.5 convolution_convert_fusion.3
  489.3 5.6 convolution_convert_fusion
  496.0 4.3 convolution_convert_fusion.1
  501.5 4.4 convolution_convert_fusion.2
  505.8 21.1 %reduce-scatter.26.cloned.1.call-done = bf16[512,256]{1,0:T(8,128)(2,1)} async-done(((bf16[512,2048]{1,0:T(8,128)(2,1)}), bf16[512,256]{1,0:T(8,128)(2,1)}) %reduce-scatter.26.cloned.1.call-update) | async-done | bytes 262160 | tf_op jit(solution)/shard_map/reduce_scatter | solution.py:53
  527.0 1.8 convert_element_type.186
  528.8 28.2 %reduce-scatter.16.cloned.1.call-done = bf16[64,2048]{1,0:T(8,128)(2,1)} async-done(((bf16[256,2048]{1,0:T(8,128)(2,1)}), bf16[64,2048]{1,0:T(8,128)(2,1)}) %reduce-scatter.16.cloned.1.call-update) | async-done | bytes 262160 | tf_op jit(solution)/shard_map/reduce_scatter | solution.py:42
  557.0 2.4 fusion.35
  559.4 35.9 %reduce-scatter.34.cloned.1.call-done = f32[256,2]{1,0:T(8,128)} async-done(((f32[2048,2]{1,0:T(8,128)}), f32[256,2]{1,0:T(8,128)}) %reduce-scatter.34.cloned.1.call-update) | async-done | bytes 2064
  596.3 11.7 %psum.8 = f32[2,256]{1,0:T(2,128)S(1)} all-reduce(f32[2,256]{1,0:T(2,128)S(1)} %copy.113), channel_id=1, replica_groups=mesh['fsdp'=2,'context'=4,'tensor'=4] {'tensor'}, use_global_device_ids=true, to_apply=%region_15.16 | all-reduce | flops 512 | bytes 4096 | tf_op jit(solution)/shard_map/psum | solution.py:204
  608.6 33.6 %reduce-scatter.24.cloned.1.call-done = bf16[256,640]{1,0:T(8,128)(2,1)} async-done(((bf16[2048,640]{1,0:T(8,128)(2,1)}), bf16[256,640]{1,0:T(8,128)(2,1)}) %reduce-scatter.24.cloned.1.call-update) | async-done | bytes 327696 | tf_op jit(solution)/shard_map/reduce_scatter | solution.py:53
  644.6 1.8 slice.98
  646.4 58.1 %reduce-scatter.32.cloned.1.call-done = bf16[1408,256]{1,0:T(8,128)(2,1)} async-done(((bf16[1408,2048]{1,0:T(8,128)(2,1)}), bf16[1408,256]{1,0:T(8,128)(2,1)}) %reduce-scatter.32.cloned.1.call-update) | async-done | bytes 720912 | tf_op jit(solution)/shard_map/reduce_scatter | solution.py:53
  704.5 2.3 convert_element_type.192
  706.8 60.6 %reduce-scatter.30.cloned.1.call-done = bf16[256,1408]{1,0:T(8,128)(2,1)} async-done(((bf16[2048,1408]{1,0:T(8,128)(2,1)}), bf16[256,1408]{1,0:T(8,128)(2,1)}) %reduce-scatter.30.cloned.1.call-update) | async-done | bytes 720912 | tf_op jit(solution)/shard_map/reduce_scatter | solution.py:53
  767.4 2.3 convert_element_type.190
  769.7 60.1 %reduce-scatter.28.cloned.1.call-done = bf16[256,1408]{1,0:T(8,128)(2,1)} async-done(((bf16[2048,1408]{1,0:T(8,128)(2,1)}), bf16[256,1408]{1,0:T(8,128)(2,1)}) %reduce-scatter.28.cloned.1.call-update) | async-done | bytes 720912 | tf_op jit(solution)/shard_map/reduce_scatter | solution.py:53
  829.8 2.3 convert_element_type.188
  (117 shorter events, 20.6 us)
Async XLA Ops:
  7.2 42.4 %all-gather.12.cloned.1.call-start = ((), (), s32[]{:S(2)}) async-start(), calls=%async_computation.11 | async-start | bytes 1310720 | tf_op jit(solution)/shard_map/all_gather | solution.py:38
  21.2 60.5 %all-gather.14.cloned.1.call-start = ((), (), s32[]{:S(2)}) async-start(), calls=%async_computation.12 | async-start | bytes 2949120 | tf_op jit(solution)/shard_map/all_gather | solution.py:49
  24.8 87.0 %all-gather.16.cloned.1.call-start = ((), (), s32[]{:S(2)}) async-start(), calls=%async_computation.13 | async-start | bytes 2359296 | tf_op jit(solution)/shard_map/all_gather | solution.py:49
  25.5 116.9 %reduce-scatter.14.cloned.1.call-start = ((), (), s32[]{:S(2)}) async-start(), calls=%async_computation.14 | async-start | bytes 1310720 | tf_op jit(solution)/shard_map/reduce_scatter | solution.py:42
  100.8 14.4 %copy-start.15 = (bf16[256]{0:T(256)(128)(2,1)S(1)}, bf16[256]{0:T(256)(128)(2,1)}, u32[]{:S(2)}) copy-start(bf16[256]{0:T(256)(128)(2,1)} %param.21) | copy-start | bytes 1540
  100.8 41.6 %copy-start.1 = (bf16[1,64,2048]{2,1,0:T(8,128)(2,1)S(1)}, bf16[1,64,2048]{2,1,0:T(8,128)(2,1)}, u32[]{:S(2)}) copy-start(bf16[1,64,2048]{2,1,0:T(8,128)(2,1)} %param.13) | copy-start | bytes 786436
  100.8 46.7 %copy-start.5 = (bf16[1,64,2048]{2,1,0:T(8,128)(2,1)S(1)}, bf16[1,64,2048]{2,1,0:T(8,128)(2,1)}, u32[]{:S(2)}) copy-start(bf16[1,64,2048]{2,1,0:T(8,128)(2,1)} %param.25) | copy-start | bytes 786436
  115.1 57.0 %all-gather.18.cloned.1.call-start = ((), (), s32[]{:S(2)}) async-start(), calls=%async_computation.15 | async-start | bytes 1310720 | tf_op jit(solution)/shard_map/all_gather | solution.py:38
  145.4 71.5 %all-gather.22.cloned.1.call-start = ((), (), s32[]{:S(2)}) async-start(), calls=%async_computation.17 | async-start | bytes 6488064 | tf_op jit(solution)/shard_map/all_gather | solution.py:49
  145.9 116.3 %all-gather.20.cloned.1.call-start = ((), (), s32[]{:S(2)}) async-start(), calls=%async_computation.16 | async-start | bytes 6488064 | tf_op jit(solution)/shard_map/all_gather | solution.py:49
  146.7 145.7 %all-gather.26.cloned.1.call-start = ((), (), s32[]{:S(2)}) async-start(), calls=%async_computation.20 | async-start | bytes 1310720 | tf_op jit(solution)/shard_map/all_gather | solution.py:38
  148.3 190.0 %all-gather.24.cloned.1.call-start = ((), (), s32[]{:S(2)}) async-start(), calls=%async_computation.18 | async-start | bytes 6488064 | tf_op jit(solution)/shard_map/all_gather | solution.py:49
  149.1 230.2 %reduce-scatter.18.cloned.1.call-start = ((), (), s32[]{:S(2)}) async-start(), calls=%async_computation.21 | async-start | bytes 1310720 | tf_op jit(solution)/shard_map/reduce_scatter | solution.py:42
  172.1 90.1 %copy-start.2 = (bf16[256,2048]{1,0:T(8,128)(2,1)S(1)}, bf16[256,2048]{1,0:T(8,128)(2,1)}, u32[]{:S(2)}) copy-start(bf16[256,2048]{1,0:T(8,128)(2,1)} %all-gather.18.cloned.1.call-done) | copy-start | bytes 3145732
  338.3 6.3 copy-start.14
  344.6 1.9 copy-start.9
  344.6 1.9 copy-start.11
  344.6 115.5 %copy-start.7 = (bf16[256,1408]{1,0:T(8,128)(2,1)}, bf16[256,1408]{1,0:T(8,128)(2,1)S(1)}, u32[]{:S(2)}) copy-start(bf16[256,1408]{1,0:T(8,128)(2,1)S(1)} %get-tuple-element.61) | copy-start | bytes 2162692
  346.4 32.8 %copy-start.3 = (bf16[64,2048]{1,0:T(8,128)(2,1)S(1)}, bf16[64,2048]{1,0:T(8,128)(2,1)}, u32[]{:S(2)}) copy-start(bf16[64,2048]{1,0:T(8,128)(2,1)} %reduce-scatter.14.cloned.1.call-done) | copy-start | bytes 786436
  352.0 57.3 %all-gather.28.cloned.1.call-start = ((), (), s32[]{:S(2)}) async-start(), calls=%async_computation.22 | async-start | bytes 1310720 | tf_op jit(solution)/shard_map/all_gather | solution.py:38
  382.5 68.5 %reduce-scatter.20.cloned.1.call-start = ((), (), s32[]{:S(2)}) async-start(), calls=%async_computation.23 | async-start | bytes 655360 | tf_op jit(solution)/shard_map/reduce_scatter | solution.py:156
  414.4 4.9 copy-start.13
  414.4 9.8 %slice-start = ((s8[8388608]{0:T(1024)(128)(4,1)}), s8[4194304]{0:T(1024)(128)(4,1)S(1)}, s32[]{:S(2)}) async-start(s8[8388608]{0:T(1024)(128)(4,1)} %bitcast.139), calls=%async_computation.31 | async-start | bytes 8388608
  419.4 4.9 slice-start.1
  425.5 1.9 copy-start
  429.7 54.3 %reduce-scatter.22.cloned.1.call-start = ((), (), s32[]{:S(2)}) async-start(), calls=%async_computation.24 | async-start | bytes 1310720 | tf_op jit(solution)/shard_map/reduce_scatter | solution.py:42
  456.7 70.3 %reduce-scatter.26.cloned.1.call-start = ((), (), s32[]{:S(2)}) async-start(), calls=%async_computation.26 | async-start | bytes 2359296 | tf_op jit(solution)/shard_map/reduce_scatter | solution.py:53
  460.1 96.9 %reduce-scatter.16.cloned.1.call-start = ((), (), s32[]{:S(2)}) async-start(), calls=%async_computation.19 | async-start | bytes 1310720 | tf_op jit(solution)/shard_map/reduce_scatter | solution.py:42
  465.5 21.1 %copy-start.4 = (bf16[256,2048]{1,0:T(8,128)(2,1)S(1)}, bf16[256,2048]{1,0:T(8,128)(2,1)}, u32[]{:S(2)}) copy-start(bf16[256,2048]{1,0:T(8,128)(2,1)} %all-gather.12.cloned.1.call-done) | copy-start | bytes 3145732
  465.6 129.7 %reduce-scatter.34.cloned.1.call-start = ((), (), s32[]{:S(2)}) async-start(), calls=%async_computation.30 | async-start | bytes 1179648
  486.6 155.5 %reduce-scatter.24.cloned.1.call-start = ((), (), s32[]{:S(2)}) async-start(), calls=%async_computation.25 | async-start | bytes 2949120 | tf_op jit(solution)/shard_map/reduce_scatter | solution.py:53
  489.2 215.3 %reduce-scatter.32.cloned.1.call-start = ((), (), s32[]{:S(2)}) async-start(), calls=%async_computation.29 | async-start | bytes 6488064 | tf_op jit(solution)/shard_map/reduce_scatter | solution.py:53
  494.9 1.1 copy-start.12
  494.9 272.5 %reduce-scatter.30.cloned.1.call-start = ((), (), s32[]{:S(2)}) async-start(), calls=%async_computation.28 | async-start | bytes 6488064 | tf_op jit(solution)/shard_map/reduce_scatter | solution.py:53
  500.3 1.1 copy-start.10
  500.4 329.4 %reduce-scatter.28.cloned.1.call-start = ((), (), s32[]{:S(2)}) async-start(), calls=%async_computation.27 | async-start | bytes 6488064 | tf_op jit(solution)/shard_map/reduce_scatter | solution.py:53
  505.8 51.2 %copy-start.6 = (bf16[64,2048]{1,0:T(8,128)(2,1)S(1)}, bf16[64,2048]{1,0:T(8,128)(2,1)}, u32[]{:S(2)}) copy-start(bf16[64,2048]{1,0:T(8,128)(2,1)} %reduce-scatter.18.cloned.1.call-done) | copy-start | bytes 786436
  505.8 51.2 %copy-start.8 = (bf16[64,2048]{1,0:T(8,128)(2,1)S(1)}, bf16[64,2048]{1,0:T(8,128)(2,1)}, u32[]{:S(2)}) copy-start(bf16[64,2048]{1,0:T(8,128)(2,1)} %reduce-scatter.22.cloned.1.call-done) | copy-start | bytes 786436
Sparse Core Ops, SparseCore 0:
  21.3 28.2 all-gather.11
  52.0 29.6 all-gather.13
  83.6 28.1 all-gather.15
  115.2 27.1 reduce-scatter.13
  145.5 26.5 all-gather.17
  174.0 42.7 all-gather.21
  218.9 43.3 all-gather.19
  264.5 27.9 all-gather.25
  294.5 43.8 all-gather.23
  352.1 27.1 reduce-scatter.17
  382.6 26.5 all-gather.27
  429.8 21.1 reduce-scatter.19
  456.8 27.1 reduce-scatter.21
  487.1 39.8 reduce-scatter.25
  529.8 27.1 reduce-scatter.15
  560.6 34.6 reduce-scatter.33
  598.5 43.6 reduce-scatter.23
  645.5 59.0 reduce-scatter.31
  708.4 59.0 reduce-scatter.29
  770.7 59.0 reduce-scatter.27
where the time goes:
time: 840 us; the launch traced here: 839 us
  waiting for transfers between devices  650 us (77%)
  matrix products  87.3 us (10%)
  blocking collectives  36.7 us (4%)
  other arithmetic  30.9 us (4%)
  local copies, waits for them, and re-layouts  18.2 us (2%)
  between operations  14.8 us (2%)
    reduce_scatter x5, waiting for transfers between devices, scatter_g(): lax.psum_scatter(g.astype(BF), FC, scatter_dimension=axis, tiled=True)  234 us
    all_gather x5, waiting for transfers between devices, gather_w(): return lax.all_gather(w, FC, axis=axis, tiled=True)  173 us
    all_gather x4, waiting for transfers between devices, rows_gather(): return lax.all_gather(x, 'tensor', axis=0, tiled=True)  93.7 us
    reduce_scatter x4, waiting for transfers between devices, rows_sum(): lax.psum_scatter(x.astype(BF), 'tensor', scatter_dimension=0, tiled=True)  92.2 us
    dot_general x15, matrix products, mm(): lax.dot_general(a, b, (((ca,), (cb,)), ((), ())), preferred_element_type=...  64 us
    unnamed x21, waiting for transfers between devices  38.8 us
    all_gather x2, blocking collectives, gather_w(): return lax.all_gather(w, FC, axis=axis, tiled=True)  19.2 us
    reduce_scatter x1, waiting for transfers between devices, one_sequence(): lax.psum_scatter(jnp.concatenate([g_k, g_v], axis=1), 'context', scatter_...  18.1 us
  transfers between devices with their start and end apart: 20, of which 20 were waited for; matrix products, arithmetic and copies ran while one was open for 10% of the time, Pallas kernels for 0%

commit v1 on v0

--- a/solution.py
+++ b/solution.py
@@ -8,6 +8,28 @@
 NEG = -1e30
 BF = jnp.bfloat16
 F32 = jnp.float32
+
+
+def joined_along(pieces, dim):
+    pieces = jnp.moveaxis(pieces, 0, dim)
+    lengths = pieces.shape
+    return pieces.reshape(*lengths[:dim], lengths[dim] * lengths[dim + 1], *lengths[dim + 2 :])
+
+
+def collect(x, axis, dim):
+    count = lax.axis_size(axis)
+    pairs = [(i, (i + 1) % count) for i in range(count)]
+    back = [(b, a) for a, b in pairs]
+    lower, upper = ([], [])
+    for hop in range(count - 1):
+        if hop % 2 == 0:
+            lower.append(lax.ppermute(lower[-1] if lower else x, axis, pairs))
+        else:
+            upper.append(lax.ppermute(upper[-1] if upper else x, axis, back))
+    blocks = jnp.stack([*lower[::-1], x, *upper])
+    shift = lax.axis_index(axis) - len(lower)
+    blocks = blocks[(jnp.arange(count) - shift) % count]
+    return joined_along(blocks, dim)
 
 
 def rope_tables(positions, head_size):
@@ -35,7 +57,7 @@
 
 
 def rows_gather(x):
-    return lax.all_gather(x, "tensor", axis=0, tiled=True)
+    return collect(x, "tensor", 0)
 
 
 def rows_sum(x):

time: 840 us -> 742 us (0.88)
  waiting for transfers between devices: 650 us -> 521 us
  starting transfers between devices: 1.48 us -> 19.3 us
    all_gather x4 -> x0, waiting for transfers between devices: 93.7 us -> none  [rows_gather(): return lax.all_gather(x, 'tensor', axis=0, tiled=True)]
    all_gather x5, waiting for transfers between devices: 173 us -> 87.7 us  [gather_w(): return lax.all_gather(w, FC, axis=axis, tiled=True)]
    ppermute x0 -> x12, waiting for transfers between devices: none -> 53.8 us  [the longest x8 46.2 us: collect(): lower.append(lax.ppermute(lower[-1] if lower else x, axis, pairs))]
    reduce_scatter x4, waiting for transfers between devices: 92.2 us -> 69.2 us  [rows_sum(): lax.psum_scatter(x.astype(BF), 'tensor', scatter_dimension=0, tiled=True)]
    reduce_scatter x5, waiting for transfers between devices: 234 us -> 254 us  [scatter_g(): lax.psum_scatter(g.astype(BF), FC, scatter_dimension=axis, tiled=True)]
    ppermute x0 -> x12, starting transfers between devices: none -> 18.4 us  [the longest x4 14.5 us: collect(): upper.append(lax.ppermute(upper[-1] if upper else x, axis, back))]
    unnamed x21 -> x17, waiting for transfers between devices: 38.8 us -> 39.7 us
  transfers between devices with their start and end apart: 20 -> 28, of which waited for: 20 -> 25; matrix products, arithmetic and copies ran while one was open for 10% -> 12% of each run, Pallas kernels for 0% -> 0%
where the time goes in v1:
time: 742 us; the launch traced here: 741 us
  waiting for transfers between devices  521 us (70%)
  matrix products  87.7 us (12%)
  blocking collectives  37.4 us (5%)
  other arithmetic  35 us (5%)
  local copies, waits for them, and re-layouts  26 us (4%)
  starting transfers between devices  19.3 us (3%)
  between operations  14.7 us (2%)
    reduce_scatter x5, waiting for transfers between devices, scatter_g(): lax.psum_scatter(g.astype(BF), FC, scatter_dimension=axis, tiled=True)  254 us
    all_gather x5, waiting for transfers between devices, gather_w(): return lax.all_gather(w, FC, axis=axis, tiled=True)  87.7 us
    reduce_scatter x4, waiting for transfers between devices, rows_sum(): lax.psum_scatter(x.astype(BF), 'tensor', scatter_dimension=0, tiled=True)  69.2 us
    dot_general x15, matrix products, mm(): lax.dot_general(a, b, (((ca,), (cb,)), ((), ())), preferred_element_type=...  64.4 us
    ppermute x8, waiting for transfers between devices, collect(): lower.append(lax.ppermute(lower[-1] if lower else x, axis, pairs))  46.2 us
    unnamed x17, waiting for transfers between devices  39.7 us
    all_gather x2, blocking collectives, gather_w(): return lax.all_gather(w, FC, axis=axis, tiled=True)  19.2 us
    reduce_scatter x1, waiting for transfers between devices, one_sequence(): lax.psum_scatter(jnp.concatenate([g_k, g_v], axis=1), 'context', scatter_...  16.7 us
  transfers between devices with their start and end apart: 28, of which 25 were waited for; matrix products, arithmetic and copies ran while one was open for 12% of the time, Pallas kernels for 0%

profile of v1, /device:TPU:0, one launch (start us, length us, event | category | flops | bytes accessed | tf_op | source)
XLA Modules:
  0.0 740.7 jit_solution(16984137720217957004)
XLA Ops:
  9.0 1.8 pad_maximum_fusion.5
  11.5 10.3 %all-gather = bf16[8,1,256]{2,1,0:T(2,128)(2,1)S(1)} all-gather(bf16[1,1,256]{2,1,0:T(2,128)(2,1)S(1)} %reshape.465), channel_id=1, replica_groups=mesh['fsdp'=2,'context'=4,'tensor'=4] {'fsdp','context'}, dimensions={0}, use_global_device_ids=true | all-gather | bytes 4608 | tf_op jit(solution)/shard_map/all_gather | solution.py:71
  24.0 3.7 collective-permute-start.2
  32.1 8.2 %collective-permute-done = bf16[64,2048]{1,0:T(8,128)(2,1)S(1)} collective-permute-done((bf16[64,2048]{1,0:T(8,128)(2,1)S(1)}, bf16[64,2048]{1,0:T(8,128)(2,1)S(1)}, u32[]{:S(2)}, u32[]{:S(2)}) %collective-permute-start) | collective-permute-done | bytes 262176 | tf_op jit(solution)/shard_map/ppermute | solution.py:26
  43.6 6.2 collective-permute-done.1
  50.6 2.8 fusion.93
  54.4 6.5 all_gather.26
  61.0 4.8 fusion.92
  66.4 4.3 fusion.14
  70.8 3.0 all-gather.10.cloned.1.call-done
  73.8 3.3 convolution_convert_fusion.5
  81.4 8.8 %all-gather.1 = bf16[8,1,256]{2,1,0:T(2,128)(2,1)S(1)} all-gather(bf16[1,1,256]{2,1,0:T(2,128)(2,1)S(1)} %reshape.467), channel_id=1, replica_groups=mesh['fsdp'=2,'context'=4,'tensor'=4] {'fsdp','context'}, dimensions={0}, use_global_device_ids=true | all-gather | bytes 4608 | tf_op jit(solution)/shard_map/all_gather | solution.py:71
  90.2 17.7 %reduce-scatter.14.cloned.1.call-done = bf16[64,2048]{1,0:T(8,128)(2,1)} async-done(((bf16[256,2048]{1,0:T(8,128)(2,1)}), bf16[64,2048]{1,0:T(8,128)(2,1)}) %reduce-scatter.14.cloned.1.call-update) | async-done | bytes 262160 | tf_op jit(solution)/shard_map/reduce_scatter | solution.py:64
  110.8 3.3 collective-permute-start.8
  114.1 3.8 collective-permute-start.5
  117.9 3.5 collective-permute-done.3
  121.5 4.6 collective-permute-done.8
  126.0 6.5 collective-permute-done.7
  135.8 7.2 collective-permute-done.4
  143.0 2.2 pad_maximum_fusion.1
  145.2 2.0 gather_fusion.1
  147.2 4.2 all-gather.14.cloned.1.call-done
  151.4 5.5 fusion.95
  156.9 39.7 %all-gather.12.cloned.1.call-done = bf16[2048,1408]{1,0:T(8,128)(2,1)} async-done(((bf16[256,1408]{1,0:T(8,128)(2,1)}), bf16[2048,1408]{1,0:T(8,128)(2,1)}) %all-gather.12.cloned.1.call-update) | async-done | bytes 5767184 | tf_op jit(solution)/shard_map/all_gather | solution.py:71
  196.6 5.5 fusion.94
  202.2 40.7 %all-gather.16.cloned.1.call-done = bf16[1408,2048]{1,0:T(8,128)(2,1)} async-done(((bf16[1408,256]{1,0:T(8,128)(2,1)}), bf16[1408,2048]{1,0:T(8,128)(2,1)}) %all-gather.16.cloned.1.call-update) | async-done | bytes 5767184 | tf_op jit(solution)/shard_map/all_gather | solution.py:71
  242.9 7.1 multiply_convert_fusion
  250.0 1.8 fusion.96
  251.9 5.5 fusion.8
  257.5 27.2 %reduce-scatter.18.cloned.1.call-done = bf16[64,2048]{1,0:T(8,128)(2,1)} async-done(((bf16[256,2048]{1,0:T(8,128)(2,1)}), bf16[64,2048]{1,0:T(8,128)(2,1)}) %reduce-scatter.18.cloned.1.call-update) | async-done | bytes 262160 | tf_op jit(solution)/shard_map/reduce_scatter | solution.py:64
  284.7 1.8 fusion.42
  288.4 3.8 collective-permute-start.11
  292.2 7.2 collective-permute-done.9
  299.4 2.6 collective-permute-done.11
  301.9 7.4 collective-permute-done.10
  310.4 2.9 gather_fusion.3
  313.4 3.4 convolution_convert_fusion.8
  317.9 4.9 fusion.17
  322.8 4.8 fusion.1
  329.0 1.9 copy-done
  333.3 3.1 fusion.13
  336.4 16.7 %reduce-scatter.20.cloned.1.call-done = f32[256,128]{0,1:T(8,128)} async-done(((f32[1024,128]{0,1:T(8,128)}), f32[256,128]{0,1:T(8,128)}) %reduce-scatter.20.cloned.1.call-update) | async-done | bytes 131088 | tf_op jit(solution)/shard_map/reduce_scatter | solution.py:178
  355.1 3.7 convolution_convert_fusion.6
  358.9 5.7 convolution_convert_fusion.7
  364.7 3.3 convolution_convert_fusion.4
  368.1 18.1 %reduce-scatter.22.cloned.1.call-done = bf16[64,2048]{1,0:T(8,128)(2,1)} async-done(((bf16[256,2048]{1,0:T(8,128)(2,1)}), bf16[64,2048]{1,0:T(8,128)(2,1)}) %reduce-scatter.22.cloned.1.call-update) | async-done | bytes 262160 | tf_op jit(solution)/shard_map/reduce_scatter | solution.py:64
  388.9 2.5 convolution_convert_fusion.3
  391.5 5.6 convolution_convert_fusion
  398.2 4.3 convolution_convert_fusion.1
  403.7 4.3 convolution_convert_fusion.2
  408.0 6.1 reduce-scatter.16.cloned.1.call-done
  414.1 2.4 fusion.38
  416.5 41.2 %reduce-scatter.26.cloned.1.call-done = bf16[512,256]{1,0:T(8,128)(2,1)} async-done(((bf16[512,2048]{1,0:T(8,128)(2,1)}), bf16[512,256]{1,0:T(8,128)(2,1)}) %reduce-scatter.26.cloned.1.call-update) | async-done | bytes 262160 | tf_op jit(solution)/shard_map/reduce_scatter | solution.py:75
  457.7 1.8 convert_element_type.204
  459.5 37.9 %reduce-scatter.34.cloned.1.call-done = f32[256,2]{1,0:T(8,128)} async-done(((f32[2048,2]{1,0:T(8,128)}), f32[256,2]{1,0:T(8,128)}) %reduce-scatter.34.cloned.1.call-update) | async-done | bytes 2064
  498.3 11.7 %psum.8 = f32[2,256]{1,0:T(2,128)S(1)} all-reduce(f32[2,256]{1,0:T(2,128)S(1)} %copy.113), channel_id=1, replica_groups=mesh['fsdp'=2,'context'=4,'tensor'=4] {'tensor'}, use_global_device_ids=true, to_apply=%region_15.16 | all-reduce | flops 512 | bytes 4096 | tf_op jit(solution)/shard_map/psum | solution.py:226
  510.6 33.7 %reduce-scatter.24.cloned.1.call-done = bf16[256,640]{1,0:T(8,128)(2,1)} async-done(((bf16[2048,640]{1,0:T(8,128)(2,1)}), bf16[256,640]{1,0:T(8,128)(2,1)}) %reduce-scatter.24.cloned.1.call-update) | async-done | bytes 327696 | tf_op jit(solution)/shard_map/reduce_scatter | solution.py:75
  546.8 1.8 slice.106
  548.6 58.2 %reduce-scatter.32.cloned.1.call-done = bf16[1408,256]{1,0:T(8,128)(2,1)} async-done(((bf16[1408,2048]{1,0:T(8,128)(2,1)}), bf16[1408,256]{1,0:T(8,128)(2,1)}) %reduce-scatter.32.cloned.1.call-update) | async-done | bytes 720912 | tf_op jit(solution)/shard_map/reduce_scatter | solution.py:75
  606.7 2.3 convert_element_type.210
  609.0 60.4 %reduce-scatter.30.cloned.1.call-done = bf16[256,1408]{1,0:T(8,128)(2,1)} async-done(((bf16[2048,1408]{1,0:T(8,128)(2,1)}), bf16[256,1408]{1,0:T(8,128)(2,1)}) %reduce-scatter.30.cloned.1.call-update) | async-done | bytes 720912 | tf_op jit(solution)/shard_map/reduce_scatter | solution.py:75
  669.5 2.3 convert_element_type.208
  671.8 60.1 %reduce-scatter.28.cloned.1.call-done = bf16[256,1408]{1,0:T(8,128)(2,1)} async-done(((bf16[2048,1408]{1,0:T(8,128)(2,1)}), bf16[256,1408]{1,0:T(8,128)(2,1)}) %reduce-scatter.28.cloned.1.call-update) | async-done | bytes 720912 | tf_op jit(solution)/shard_map/reduce_scatter | solution.py:75
  731.9 2.3 convert_element_type.206
  (185 shorter events, 43.9 us)
Async XLA Ops:
  7.2 43.4 %all-gather.8.cloned.1.call-start = ((), (), s32[]{:S(2)}) async-start(), calls=%async_computation.11 | async-start | bytes 2949120 | tf_op jit(solution)/shard_map/all_gather | solution.py:71
  10.8 63.1 %all-gather.10.cloned.1.call-start = ((), (), s32[]{:S(2)}) async-start(), calls=%async_computation.12 | async-start | bytes 2359296 | tf_op jit(solution)/shard_map/all_gather | solution.py:71
  22.9 8.3 %copy-start.27 = (f32[64]{0:T(128)}, f32[64]{0:T(128)S(1)}, u32[]{:S(2)}) copy-start(f32[64]{0:T(128)S(1)} %add_rsqrt_fusion.1) | copy-start | bytes 772
  24.0 19.5 %collective-permute-start.2 = (bf16[64,2048]{1,0:T(8,128)(2,1)S(1)}, bf16[64,2048]{1,0:T(8,128)(2,1)S(1)}, u32[]{:S(2)}, u32[]{:S(2)}) collective-permute-start(bf16[64,2048]{1,0:T(8,128)(2,1)S(1)} %fusion.43), channel_id=1, source_target_pairs={{1,0},{2,1},{3,2},{0,3},{5,4},{6,5},{7,6},{4,7},{9,8},{10,9},{11,1... | collective-permute-start | bytes 786440 | tf_op jit(solution)/shard_map/ppermute | solution.py:28
  27.7 12.6 %collective-permute-start = (bf16[64,2048]{1,0:T(8,128)(2,1)S(1)}, bf16[64,2048]{1,0:T(8,128)(2,1)S(1)}, u32[]{:S(2)}, u32[]{:S(2)}) collective-permute-start(bf16[64,2048]{1,0:T(8,128)(2,1)S(1)} %fusion.43), channel_id=1, source_target_pairs={{0,1},{1,2},{2,3},{3,0},{4,5},{5,6},{6,7},{7,4},{8,9},{9,10},{10,1... | collective-permute-start | bytes 786440 | tf_op jit(solution)/shard_map/ppermute | solution.py:26
  27.7 80.2 %reduce-scatter.14.cloned.1.call-start = ((), (), s32[]{:S(2)}) async-start(), calls=%async_computation.13 | async-start | bytes 1310720 | tf_op jit(solution)/shard_map/reduce_scatter | solution.py:64
  29.6 23.7 %copy-start.21 = (s32[1024]{0:T(1024)}, s32[1024]{0:T(1024)S(1)}, u32[]{:S(2)}) copy-start(s32[1024]{0:T(1024)S(1)} %pad_clamp_fusion) | copy-start | bytes 12292
  31.2 22.6 %copy-start.19 = (f32[256]{0:T(256)}, f32[256]{0:T(256)S(1)}, u32[]{:S(2)}) copy-start(f32[256]{0:T(256)S(1)} %subtract_convert_fusion.2) | copy-start | bytes 3076
  31.3 22.6 %copy-start.32 = (f32[32]{0:T(128)}, f32[32]{0:T(128)S(1)}, u32[]{:S(2)}) copy-start(f32[32]{0:T(128)S(1)} %multiply_exponential_fusion) | copy-start | bytes 388
  32.1 28.8 %copy-start.14 = (f32[256,32]{0,1:T(8,128)}, f32[256,32]{0,1:T(8,128)S(1)}, u32[]{:S(2)}) copy-start(f32[256,32]{0,1:T(8,128)S(1)} %get-tuple-element.78) | copy-start | bytes 98308
  40.3 9.5 %collective-permute-start.1 = (bf16[64,2048]{1,0:T(8,128)(2,1)S(1)}, bf16[64,2048]{1,0:T(8,128)(2,1)S(1)}, u32[]{:S(2)}, u32[]{:S(2)}) collective-permute-start(bf16[64,2048]{1,0:T(8,128)(2,1)S(1)} %collective-permute-done), channel_id=1, source_target_pairs={{0,1},{1,2},{2,3},{3,0},{4,5},{5,6},{6,7},{7,4},{8,9},{9,10},{10,1... | collective-permute-start | bytes 786440 | tf_op jit(solution)/shard_map/ppermute | solution.py:26
  61.0 4.8 copy-start.12
  70.8 39.4 %copy-start.6 = (bf16[64,8,256]{2,0,1:T(8,128)(2,1)}, bf16[64,8,256]{2,0,1:T(8,128)(2,1)S(1)}, u32[]{:S(2)}) copy-start(bf16[64,8,256]{2,0,1:T(8,128)(2,1)S(1)} %fusion.14) | copy-start | bytes 786436
  70.8 8.9 %copy-start.3 = (bf16[1,64,2048]{2,1,0:T(8,128)(2,1)S(1)}, bf16[1,64,2048]{2,1,0:T(8,128)(2,1)}, u32[]{:S(2)}) copy-start(bf16[1,64,2048]{2,1,0:T(8,128)(2,1)} %param.25) | copy-start | bytes 786436
  70.8 10.6 %copy-start.37 = (bf16[256]{0:T(256)(128)(2,1)S(1)}, bf16[256]{0:T(256)(128)(2,1)}, u32[]{:S(2)}) copy-start(bf16[256]{0:T(256)(128)(2,1)} %param.21) | copy-start | bytes 1540
  70.8 37.1 %copy-start.1 = (bf16[1,64,2048]{2,1,0:T(8,128)(2,1)S(1)}, bf16[1,64,2048]{2,1,0:T(8,128)(2,1)}, u32[]{:S(2)}) copy-start(bf16[1,64,2048]{2,1,0:T(8,128)(2,1)} %param.13) | copy-start | bytes 786436
  77.2 74.2 %all-gather.14.cloned.1.call-start = ((), (), s32[]{:S(2)}) async-start(), calls=%async_computation.15 | async-start | bytes 6488064 | tf_op jit(solution)/shard_map/all_gather | solution.py:71
  77.7 118.9 %all-gather.12.cloned.1.call-start = ((), (), s32[]{:S(2)}) async-start(), calls=%async_computation.14 | async-start | bytes 6488064 | tf_op jit(solution)/shard_map/all_gather | solution.py:71
  78.3 164.6 %all-gather.16.cloned.1.call-start = ((), (), s32[]{:S(2)}) async-start(), calls=%async_computation.16 | async-start | bytes 6488064 | tf_op jit(solution)/shard_map/all_gather | solution.py:71
  78.9 205.8 %reduce-scatter.18.cloned.1.call-start = ((), (), s32[]{:S(2)}) async-start(), calls=%async_computation.18 | async-start | bytes 1310720 | tf_op jit(solution)/shard_map/reduce_scatter | solution.py:64
  79.7 52.8 %copy-start.24 = (f32[64]{0:T(128)}, f32[64]{0:T(128)S(1)}, u32[]{:S(2)}) copy-start(f32[64]{0:T(128)S(1)} %convert_bitcast_fusion.2) | copy-start | bytes 772
  79.8 34.2 %collective-permute-start.6 = (bf16[64,2048]{1,0:T(8,128)(2,1)S(1)}, bf16[64,2048]{1,0:T(8,128)(2,1)S(1)}, u32[]{:S(2)}, u32[]{:S(2)}) collective-permute-start(bf16[64,2048]{1,0:T(8,128)(2,1)S(1)} %fusion.50), channel_id=1, source_target_pairs={{0,1},{1,2},{2,3},{3,0},{4,5},{5,6},{6,7},{7,4},{8,9},{9,10},{10,1... | collective-permute-start | bytes 786440 | tf_op jit(solution)/shard_map/ppermute | solution.py:26
  109.1 23.4 %copy-start.29 = (f32[64]{0:T(128)}, f32[64]{0:T(128)S(1)}, u32[]{:S(2)}) copy-start(f32[64]{0:T(128)S(1)} %add_rsqrt_fusion) | copy-start | bytes 772
  110.2 11.2 %collective-permute-start.3 = (bf16[64,2048]{1,0:T(8,128)(2,1)S(1)}, bf16[64,2048]{1,0:T(8,128)(2,1)}, u32[]{:S(2)}, u32[]{:S(2)}) collective-permute-start(bf16[64,2048]{1,0:T(8,128)(2,1)S(1)} %multiply_convert_fusion.4), channel_id=1, source_target_pairs={{0,1},{1,2},{2,3},{3,0},{4,5},{5,6},{6,7},{7,4},{8,9},{9,10},{10,1... | collective-permute-start | bytes 786440 | tf_op jit(solution)/shard_map/ppermute | solution.py:26
  110.8 15.2 %collective-permute-start.8 = (bf16[64,2048]{1,0:T(8,128)(2,1)S(1)}, bf16[64,2048]{1,0:T(8,128)(2,1)S(1)}, u32[]{:S(2)}, u32[]{:S(2)}) collective-permute-start(bf16[64,2048]{1,0:T(8,128)(2,1)S(1)} %fusion.50), channel_id=1, source_target_pairs={{1,0},{2,1},{3,2},{0,3},{5,4},{6,5},{7,6},{4,7},{9,8},{10,9},{11,1... | collective-permute-start | bytes 786440 | tf_op jit(solution)/shard_map/ppermute | solution.py:28
  114.1 18.5 %copy-start.16 = (bf16[64,2048]{1,0:T(8,128)(2,1)}, bf16[64,2048]{1,0:T(8,128)(2,1)S(1)}, u32[]{:S(2)}) copy-start(bf16[64,2048]{1,0:T(8,128)(2,1)S(1)} %collective-permute-done.6) | copy-start | bytes 786436
  114.1 18.5 %collective-permute-start.7 = (bf16[64,2048]{1,0:T(8,128)(2,1)S(1)}, bf16[64,2048]{1,0:T(8,128)(2,1)S(1)}, u32[]{:S(2)}, u32[]{:S(2)}) collective-permute-start(bf16[64,2048]{1,0:T(8,128)(2,1)S(1)} %collective-permute-done.6), channel_id=1, source_target_pairs={{0,1},{1,2},{2,3},{3,0},{4,5},{5,6},{6,7},{7,4},{8,9},{9,10},{10,1... | collective-permute-start | bytes 786440 | tf_op jit(solution)/shard_map/ppermute | solution.py:26
  114.1 21.7 %collective-permute-start.5 = (bf16[64,2048]{1,0:T(8,128)(2,1)S(1)}, bf16[64,2048]{1,0:T(8,128)(2,1)}, u32[]{:S(2)}, u32[]{:S(2)}) collective-permute-start(bf16[64,2048]{1,0:T(8,128)(2,1)S(1)} %multiply_convert_fusion.4), channel_id=1, source_target_pairs={{1,0},{2,1},{3,2},{0,3},{5,4},{6,5},{7,6},{4,7},{9,8},{10,9},{11,1... | collective-permute-start | bytes 786440 | tf_op jit(solution)/shard_map/ppermute | solution.py:28
  121.3 21.7 %collective-permute-start.4 = (bf16[64,2048]{1,0:T(8,128)(2,1)}, bf16[64,2048]{1,0:T(8,128)(2,1)}, u32[]{:S(2)}, u32[]{:S(2)}) collective-permute-start(bf16[64,2048]{1,0:T(8,128)(2,1)} %collective-permute-done.3), channel_id=1, source_target_pairs={{0,1},{1,2},{2,3},{3,0},{4,5},{5,6},{6,7},{7,4},{8,9},{9,10},{10,1... | collective-permute-start | bytes 786440 | tf_op jit(solution)/shard_map/ppermute | solution.py:26
  242.9 7.1 copy-start.36
  250.0 1.8 copy-start.8
  250.0 1.8 copy-start.10
  251.9 32.9 %copy-start.2 = (bf16[64,2048]{1,0:T(8,128)(2,1)S(1)}, bf16[64,2048]{1,0:T(8,128)(2,1)}, u32[]{:S(2)}) copy-start(bf16[64,2048]{1,0:T(8,128)(2,1)} %reduce-scatter.14.cloned.1.call-done) | copy-start | bytes 786436
  251.9 32.9 %copy-start.30 = (f32[64]{0:T(128)S(1)}, f32[64]{0:T(128)}, u32[]{:S(2)}) copy-start(f32[64]{0:T(128)} %copy-done.29) | copy-start | bytes 772
  251.9 35.2 %copy-start.25 = (f32[64]{0:T(128)S(1)}, f32[64]{0:T(128)}, u32[]{:S(2)}) copy-start(f32[64]{0:T(128)} %copy-done.24) | copy-start | bytes 772
  257.4 95.7 %reduce-scatter.20.cloned.1.call-start = ((), (), s32[]{:S(2)}) async-start(), calls=%async_computation.19 | async-start | bytes 655360 | tf_op jit(solution)/shard_map/reduce_scatter | solution.py:178
  288.3 11.1 %collective-permute-start.9 = (bf16[64,2048]{1,0:T(8,128)(2,1)S(1)}, bf16[64,2048]{1,0:T(8,128)(2,1)S(1)}, u32[]{:S(2)}, u32[]{:S(2)}) collective-permute-start(bf16[64,2048]{1,0:T(8,128)(2,1)S(1)} %fusion.89), channel_id=1, source_target_pairs={{0,1},{1,2},{2,3},{3,0},{4,5},{5,6},{6,7},{7,4},{8,9},{9,10},{10,1... | collective-permute-start | bytes 786440 | tf_op jit(solution)/shard_map/ppermute | solution.py:26
  288.4 13.6 %collective-permute-start.11 = (bf16[64,2048]{1,0:T(8,128)(2,1)S(1)}, bf16[64,2048]{1,0:T(8,128)(2,1)S(1)}, u32[]{:S(2)}, u32[]{:S(2)}) collective-permute-start(bf16[64,2048]{1,0:T(8,128)(2,1)S(1)} %fusion.89), channel_id=1, source_target_pairs={{1,0},{2,1},{3,2},{0,3},{5,4},{6,5},{7,6},{4,7},{9,8},{10,9},{11,1... | collective-permute-start | bytes 786440 | tf_op jit(solution)/shard_map/ppermute | solution.py:28
  299.4 10.0 %collective-permute-start.10 = (bf16[64,2048]{1,0:T(8,128)(2,1)S(1)}, bf16[64,2048]{1,0:T(8,128)(2,1)S(1)}, u32[]{:S(2)}, u32[]{:S(2)}) collective-permute-start(bf16[64,2048]{1,0:T(8,128)(2,1)S(1)} %collective-permute-done.9), channel_id=1, source_target_pairs={{0,1},{1,2},{2,3},{3,0},{4,5},{5,6},{6,7},{7,4},{8,9},{9,10},{10,1... | collective-permute-start | bytes 786440 | tf_op jit(solution)/shard_map/ppermute | solution.py:26
  317.8 4.9 copy-start.23
  317.8 9.8 %slice-start = ((s8[8388608]{0:T(1024)(128)(4,1)}), s8[4194304]{0:T(1024)(128)(4,1)S(1)}, s32[]{:S(2)}) async-start(s8[8388608]{0:T(1024)(128)(4,1)} %bitcast.196), calls=%async_computation.27 | async-start | bytes 8388608
  322.8 4.9 slice-start.1
  327.7 3.3 copy-start.13
  329.0 2.0 copy-start
  332.3 4.0 copy-start.15
  332.3 4.0 copy-start.17
  332.3 21.7 %copy-start.20 = (f32[256]{0:T(256)S(1)}, f32[256]{0:T(256)}, u32[]{:S(2)}) copy-start(f32[256]{0:T(256)} %copy-done.19) | copy-start | bytes 3076
  332.3 21.7 %copy-start.33 = (f32[32]{0:T(128)S(1)}, f32[32]{0:T(128)}, u32[]{:S(2)}) copy-start(f32[32]{0:T(128)} %copy-done.32) | copy-start | bytes 388
  333.2 52.9 %reduce-scatter.22.cloned.1.call-start = ((), (), s32[]{:S(2)}) async-start(), calls=%async_computation.20 | async-start | bytes 1310720 | tf_op jit(solution)/shard_map/reduce_scatter | solution.py:64
  358.9 55.3 %reduce-scatter.16.cloned.1.call-start = ((), (), s32[]{:S(2)}) async-start(), calls=%async_computation.17 | async-start | bytes 1310720 | tf_op jit(solution)/shard_map/reduce_scatter | solution.py:64
  358.9 5.8 copy-start.7
  364.6 21.5 %copy-start.28 = (f32[64]{0:T(128)S(1)}, f32[64]{0:T(128)}, u32[]{:S(2)}) copy-start(f32[64]{0:T(128)} %copy-done.27) | copy-start | bytes 772
  364.6 22.8 %copy-start.18 = (f32[2048]{0:T(1024)S(1)}, f32[2048]{0:T(1024)}, u32[]{:S(2)}) copy-start(f32[2048]{0:T(1024)} %get-tuple-element.55) | copy-start | bytes 24580
  364.6 93.0 %reduce-scatter.26.cloned.1.call-start = ((), (), s32[]{:S(2)}) async-start(), calls=%async_computation.22 | async-start | bytes 2359296 | tf_op jit(solution)/shard_map/reduce_scatter | solution.py:75
  368.0 129.3 %reduce-scatter.34.cloned.1.call-start = ((), (), s32[]{:S(2)}) async-start(), calls=%async_computation.26 | async-start | bytes 1179648
  388.8 155.5 %reduce-scatter.24.cloned.1.call-start = ((), (), s32[]{:S(2)}) async-start(), calls=%async_computation.21 | async-start | bytes 2949120 | tf_op jit(solution)/shard_map/reduce_scatter | solution.py:75
  391.4 215.3 %reduce-scatter.32.cloned.1.call-start = ((), (), s32[]{:S(2)}) async-start(), calls=%async_computation.25 | async-start | bytes 6488064 | tf_op jit(solution)/shard_map/reduce_scatter | solution.py:75
  397.1 272.3 %reduce-scatter.30.cloned.1.call-start = ((), (), s32[]{:S(2)}) async-start(), calls=%async_computation.24 | async-start | bytes 6488064 | tf_op jit(solution)/shard_map/reduce_scatter | solution.py:75
  402.6 329.3 %reduce-scatter.28.cloned.1.call-start = ((), (), s32[]{:S(2)}) async-start(), calls=%async_computation.23 | async-start | bytes 6488064 | tf_op jit(solution)/shard_map/reduce_scatter | solution.py:75
  407.9 6.2 copy-start.4
  407.9 6.2 copy-start.5
  407.9 6.2 copy-start.26
  407.9 6.2 copy-start.31
  408.0 6.2 copy-start.35
  (4 other events, 3.4 us)
Sparse Core Ops, SparseCore 0:
  10.9 32.8 all-gather.7
  45.6 28.1 all-gather.9
  77.3 30.6 reduce-scatter.13
  109.8 41.5 all-gather.13
  153.3 43.3 all-gather.11
  198.5 44.3 all-gather.15
  257.6 27.1 reduce-scatter.17
  333.3 19.8 reduce-scatter.19
  359.0 27.1 reduce-scatter.21
  388.3 25.7 reduce-scatter.15
  417.8 39.8 reduce-scatter.25
  461.3 35.9 reduce-scatter.33
  500.6 43.6 reduce-scatter.23
  547.6 59.0 reduce-scatter.31
  610.4 59.0 reduce-scatter.29
  672.8 59.0 reduce-scatter.27
